TPU v7x, 512 devices: a whole 4x4x16 slice. The times are simulated.
512 devices in a mesh: seq: 64 (over z, x_hi, core), head: 8 (over x_lo, y).
Axes of the slice: x: 4 (x_hi: 2, x_lo: 2; x = x_hi * 2 + x_lo), y: 4, z: 16, core: 2. Of those that a mesh axis runs over, the one named last changes fastest.
Arguments:
- attention: bfloat16 [16, 4096, 1536], P(None, 'seq', 'head'), may hold values from -6 to 6
- encoder_skip: bfloat16 [16, 8192, 1536], P('head', 'seq'), may hold values from -6 to 6
- depth_filter: float32 [3, 1536], replicated, may hold values from -3 to 3
- point_weight: bfloat16 [1536, 1536], P('head'), may hold values from -0.15625 to 0.15625
- crop_offset: int32 [16], P('head'), may hold values from 0 to 128
- target_bins: int32 [16, 128], P('head'), may hold values from 0 to 127
- cotangent: bfloat16 [16, 8192, 1536], P('head', 'seq'), may hold values from -6 to 6
Outputs:
- target_rows: bfloat16 [16, 128, 1536], P('head', 'seq')
- attention_grad: bfloat16 [16, 4096, 1536], P('head', 'seq')
- skip_grad: bfloat16 [16, 8192, 1536], P('head', 'seq')
- filter_grad: float32 [3, 1536], replicated
Inputs may be any that keep to these rules, and one draw needn't show every extreme that they name: The cropped window of sequence b starts at bin crop_offset[b]; bins of it past the end of the sequence are empty. Target j of sequence b reads bin 128 * (j // 2) + target_bins[b, j] of the cropped window.
All inputs are finite; a program needn't handle non-finite values.
Results may differ from a plain program's by a relative error of at most 0.007.
Values may be sent and summed in bfloat16 or wider, within the bound.
A program may use at most 64 MiB of HBM per device.

v0:
```python
import math
import jax
import jax.numpy as jnp
from jax import lax
from jax.sharding import PartitionSpec as P

NTD = 2


def extended(shard, sides, width):
    for axis, dim in sides:
        count, length = (lax.axis_size(axis), shard.shape[dim])
        up = [(i, (i + 1) % count) for i in range(count - 1)]
        down = [(j, i) for i, j in up]
        last = lax.slice_in_dim(shard, length - width, length, axis=dim)
        initial = lax.slice_in_dim(shard, 0, width, axis=dim)
        before = lax.ppermute(last, axis, up)
        after = lax.ppermute(initial, axis, down)
        shard = jnp.concatenate([before, shard, after], axis=dim)
    return shard


def passed_along(shard, axis, by):
    count = lax.axis_size(axis)
    pairs = [(i, i + by) for i in range(count) if 0 <= i + by < count]
    return lax.ppermute(shard, axis, pairs)


def gelu_slope(values):
    return (
        0.5 * (1.0 + lax.erf(values * 0.7071067811865476))
        + values * jnp.exp(-0.5 * values * values) * 0.3989422804014327
    )


def with_rims(field):
    return extended(field, (("seq", 1),), 1)


def one_hot(places, length):
    return (places[:, :, None] == jnp.arange(length, dtype=jnp.int32)[None, None, :]).astype(
        jnp.bfloat16
    )


def shards(
    attention, encoder_skip, depth_filter, point_weight, crop_offset, target_bins, cotangent
):
    slab_input = lax.all_to_all(attention, "head", split_axis=0, concat_axis=2, tiled=True)
    local_seqs = encoder_skip.shape[0]
    slab_rows = encoder_skip.shape[1]
    channels = encoder_skip.shape[2]
    summed = (
        jnp.repeat(slab_input, 2, axis=1).astype(jnp.float32) + encoder_skip.astype(jnp.float32)
    ).astype(jnp.bfloat16)
    padded = with_rims(summed)
    filtered = (
        depth_filter[0] * padded[:, :-2]
        + depth_filter[1] * padded[:, 1:-1]
        + depth_filter[2] * padded[:, 2:]
    )
    activated = jax.nn.gelu(filtered, approximate=False).astype(jnp.bfloat16)
    flat_act = activated.reshape(local_seqs * slab_rows, channels)
    full_weight = lax.all_gather(point_weight, "head", axis=0, tiled=True)
    mixed_rows = jnp.dot(flat_act, full_weight, preferred_element_type=jnp.float32)
    block_out = (
        summed.astype(jnp.float32) + mixed_rows.reshape(local_seqs, slab_rows, channels)
    ).astype(jnp.bfloat16)
    slab_index = lax.axis_index("seq")
    my_places = (
        lax.dynamic_slice_in_dim(target_bins, slab_index * NTD, NTD, 1) + crop_offset[:, None]
    )
    next_block = passed_along(block_out, "seq", -1)
    joined = jnp.concatenate([block_out, next_block], axis=1)
    target_rows = jnp.einsum(
        "sjr,srd->sjd",
        one_hot(my_places, 2 * slab_rows),
        joined,
        preferred_element_type=jnp.float32,
    ).astype(jnp.bfloat16)
    prev_cot = passed_along(cotangent, "seq", 1)
    cot_pair = jnp.concatenate([prev_cot, cotangent], axis=1)

    def crop_back(cot_block, shift_by):
        return lax.dynamic_slice_in_dim(cot_block, slab_rows - shift_by, slab_rows, 0)

    grad_out = jax.vmap(crop_back)(cot_pair, crop_offset)
    flat_grad = grad_out.reshape(local_seqs * slab_rows, channels)
    grad_act = lax.dot_general(
        flat_grad, full_weight, (((1,), (1,)), ((), ())), preferred_element_type=jnp.float32
    )
    grad_conv = (grad_act.reshape(local_seqs, slab_rows, channels) * gelu_slope(filtered)).astype(
        jnp.bfloat16
    )
    grad_padded = with_rims(grad_conv)
    grad_sum = (
        grad_out.astype(jnp.float32)
        + depth_filter[0] * grad_padded[:, 2:]
        + depth_filter[1] * grad_padded[:, 1:-1]
        + depth_filter[2] * grad_padded[:, :-2]
    )
    skip_grad = grad_sum.astype(jnp.bfloat16)
    attention_grad = (
        grad_sum.reshape(local_seqs, slab_rows // 2, 2, channels).sum(axis=2).astype(jnp.bfloat16)
    )
    filter_terms = jnp.stack(
        [
            jnp.einsum(
                "srd,srd->d", grad_conv, padded[:, 0:slab_rows], preferred_element_type=jnp.float32
            ),
            jnp.einsum(
                "srd,srd->d",
                grad_conv,
                padded[:, 1 : slab_rows + 1],
                preferred_element_type=jnp.float32,
            ),
            jnp.einsum(
                "srd,srd->d",
                grad_conv,
                padded[:, 2 : slab_rows + 2],
                preferred_element_type=jnp.float32,
            ),
        ]
    )
    filter_sum = lax.psum(filter_terms, ("seq", "head"))
    row_count = local_seqs * lax.axis_size("head") * slab_rows * lax.axis_size("seq")
    filter_grad = filter_sum * (1.0 / math.sqrt(row_count))
    return (target_rows, attention_grad, skip_grad, filter_grad)


def solution(mesh):
    in_specs = (
        P(None, "seq", "head"),
        P("head", "seq", None),
        P(),
        P("head", None),
        P("head"),
        P("head", None),
        P("head", "seq", None),
    )
    out_specs = (P("head", "seq", None), P("head", "seq", None), P("head", "seq", None), P())
    return jax.shard_map(shards, mesh=mesh, in_specs=in_specs, out_specs=out_specs, check_vma=False)
```

profile of v0, /device:TPU:32, one launch (start us, length us, event | category | flops | bytes accessed | tf_op | source)
XLA Modules:
  0.0 226.0 jit_solution(16963135204489975365)
XLA Ops:
  7.2 0.7 all-gather.2.cloned.1.call-update
  7.9 5.4 %all-to-all-start = ((bf16[16,64,192]{2,1,0:T(8,128)(2,1)}), bf16[16,64,192]{2,1,0:T(8,128)(2,1)S(1)}, u32[]{:S(2)}, u32[]{:S(2)}) async-start(bf16[16,64,192]{2,1,0:T(8,128)(2,1)} %param.7), calls=%async_computation | async-start | bytes 1048576 | tf_op jit(solution)/shard_map/all_to_all | solution.py:49
  13.3 1.9 collective-permute-start.3
  15.6 7.4 %all-to-all-done = bf16[16,64,192]{2,1,0:T(8,128)(2,1)S(1)} async-done(((bf16[16,64,192]{2,1,0:T(8,128)(2,1)}), bf16[16,64,192]{2,1,0:T(8,128)(2,1)S(1)}, u32[]{:S(2)}, u32[]{:S(2)}) %all-to-all-start) | async-done | bytes 393248 | tf_op jit(solution)/shard_map/all_to_all | solution.py:49
  24.1 1.1 convert_element_type.67
  25.2 1.3 add_convert_fusion
  26.6 1.9 collective-permute-start
  28.5 6.2 %collective-permute-start.1 = (bf16[2,1,1536]{2,1,0:T(2,128)(2,1)S(1)}, bf16[2,1,1536]{2,1,0:T(2,128)(2,1)S(1)}, u32[]{:S(2)}, u32[]{:S(2)}) collective-permute-start(bf16[2,1,1536]{2,1,0:T(2,128)(2,1)S(1)} %get-tuple-element.41), channel_id=1, source_target_pairs={{8,0},{16,8},{24,16},{32,24},{40,32},{48,40},{56,48},{64,56},{72,6... | collective-permute-start | bytes 18440 | tf_op jit(solution)/shard_map/ppermute | solution.py:18
  34.7 1.5 pad_maximum_fusion
  36.2 4.0 %while.1 = (s32[]{:T(128)}, bf16[2,256,1536]{2,1,0:T(8,128)(2,1)S(1)}, s32[2,3]{1,0:T(2,128)S(1)}, bf16[2,128,1536]{2,1,0:T(8,128)(2,1)S(1)}, s32[]{:T(128)}) while((s32[]{:T(128)}, bf16[2,256,1536]{2,1,0:T(8,128)(2,1)S(1)}, s32[2,3]{1,0:T(2,128)S(1)}, bf16[2,128,1536]{2,1,0:T(8,128)(2,1)S(1)}, s32[]{:T(128)}) %tuple.38), condition=%wide.while_cond, body=%wide.while_body.sunk | while | flops 2 | bytes 786557 | solution.py:85
  36.8 1.4 dynamic-slice_dynamic-update-slice_fusion.2
  38.9 1.4 dynamic-slice_dynamic-update-slice_fusion.2
  40.9 38.8 %all-gather.2.cloned.1.call-done = bf16[1536,1536]{1,0:T(8,128)(2,1)} async-done(((bf16[192,1536]{1,0:T(8,128)(2,1)}), bf16[1536,1536]{1,0:T(8,128)(2,1)}) %all-gather.2.cloned.1.call-update) | async-done | bytes 4718608 | tf_op jit(solution)/shard_map/all_gather | solution.py:64
  79.7 8.3 %fusion.10 = bf16[2,128,1536]{2,1,0:T(8,128)(2,1)} fusion(bf16[1536,1536]{1,0:T(8,128)(2,1)} %all-gather.2.cloned.1.call-done, bf16[2,128,1536]{2,1,0:T(8,128)(2,1)S(1)} %copy-done.1, bf16[2,1,1536]{2,1,0:T(2,128)(2,1)S(1)} %collective-permute-done.1, bf16[2,1,1536]{2,1,0:T(2,128)(2,1)S(1)} %collective-permute-done, f32[1536]{0:T(1024)S(1)} %get-tuple-element.24, ...), kind=kOutput, calls=%fused_computation.8 | convolution fusion | flops 1240203264 | bytes 6322176 | tf_op jit(solution)/shard_map/dot_general | solution.py:65
  88.0 3.8 %collective-permute-start.2 = (bf16[2,128,1536]{2,1,0:T(8,128)(2,1)}, bf16[2,128,1536]{2,1,0:T(8,128)(2,1)}, u32[]{:S(2)}, u32[]{:S(2)}) collective-permute-start(bf16[2,128,1536]{2,1,0:T(8,128)(2,1)} %fusion.10), channel_id=1, source_target_pairs={{8,0},{16,8},{24,16},{32,24},{40,32},{48,40},{56,48},{64,56},{72,6... | collective-permute-start | bytes 2359304 | tf_op jit(solution)/shard_map/ppermute | solution.py:26
  91.8 2.9 %fusion.25 = (f32[1536]{0:T(1024)S(1)}, f32[1536]{0:T(1024)S(1)}, f32[1536]{0:T(1024)S(1)}, bf16[2,128,1536]{2,1,0:T(8,128)(2,1)S(1)}) fusion(bf16[2,128,1536]{2,1,0:T(8,128)(2,1)S(1)} %copy-done.1, bf16[2,1,1536]{2,1,0:T(2,128)(2,1)S(1)} %collective-permute-done, bf16[2,1,1536]{2,1,0:T(2,128)(2,1)S(1)} %collective-permute-done.1, ...), kind=kOutput, calls=%fused_computation.26 | convolution fusion | flops 1222110720 | bytes 7127040 | tf_op jit(solution)/shard_map/dot_general | solution.py:89
  94.8 105.9 %psum.7 = f32[3,1536]{1,0:T(4,128)S(1)} all-reduce(f32[3,1536]{1,0:T(4,128)S(1)} %pad_maximum_fusion.6), channel_id=1, replica_groups=mesh['seq'=64,'head'=8] {'seq','head'}, use_global_device_ids=true, to_apply=%region_1.0 | all-reduce | flops 4608 | bytes 36864 | tf_op jit(solution)/shard_map/psum | solution.py:125
  200.8 2.2 collective-permute-start.4
  203.0 2.3 %collective-permute-start.5 = (bf16[2,1,1536]{2,1,0:T(2,128)(2,1)S(1)}, bf16[2,1,1536]{2,1,0:T(2,128)(2,1)S(1)}, u32[]{:S(2)}, u32[]{:S(2)}) collective-permute-start(bf16[2,1,1536]{2,1,0:T(2,128)(2,1)S(1)} %get-tuple-element.39), channel_id=1, source_target_pairs={{0,8},{8,16},{16,24},{24,32},{32,40},{40,48},{48,56},{56,64},{64,7... | collective-permute-start | bytes 18440 | tf_op jit(solution)/shard_map/ppermute | solution.py:17
  205.9 4.5 %collective-permute-done.5 = bf16[2,1,1536]{2,1,0:T(2,128)(2,1)S(1)} collective-permute-done((bf16[2,1,1536]{2,1,0:T(2,128)(2,1)S(1)}, bf16[2,1,1536]{2,1,0:T(2,128)(2,1)S(1)}, u32[]{:S(2)}, u32[]{:S(2)}) %collective-permute-start.5) | collective-permute-done | bytes 6176 | tf_op jit(solution)/shard_map/ppermute | solution.py:17
  210.4 2.7 %fusion.111 = (bf16[2,128,1536]{2,1,0:T(8,128)(2,1)}, f32[2,128,1536]{2,1,0:T(8,128)S(1)}) fusion(bf16[2,128,1536]{2,1,0:T(8,128)(2,1)S(1)} %get-tuple-element.42, bf16[2,1,1536]{2,1,0:T(2,128)(2,1)S(1)} %collective-permute-done.5, f32[1536]{0:T(1024)S(1)} %get-tuple-element.24, f32[1536]{0:T(1024)S(1)} %get-tuple-element.25, ...), kind=kLoop, calls=%fused_computation.134 | loop fusion | flops 6684672 | bytes 3962880 | tf_op jit(solution)/shard_map/convert_element_type | solution.py:102
  213.1 0.9 reshape.30
  214.0 2.8 %reduce_sum.9 = bf16[2,64,1536]{2,1,0:T(8,128)(2,1)} reduce(f32[2,64,2,1536]{3,2,1,0:T(2,128)S(1)} %reshape.30, f32[]{:T(128)} %constant.14.clone.1), dimensions={2}, to_apply=%region_0.0 | reduce | flops 196608 | bytes 1966084 | tf_op jit(solution)/shard_map/reduce_sum | solution.py:104
  216.8 2.3 %convolution_convert_fusion = bf16[2,2,1536]{2,1,0:T(2,128)(2,1)} fusion(bf16[2,128,1536]{2,1,0:T(8,128)(2,1)} %collective-permute-done.2, bf16[2,128,1536]{2,1,0:T(8,128)(2,1)} %fusion.10, s32[2,2]{1,0:T(2,128)S(1)} %dynamic-slice_add_fusion), kind=kOutput, calls=%fused_computation.15 | convolution fusion | flops 6298624 | bytes 1585168 | tf_op jit(solution)/shard_map/sjr,srd->sjd/dot_general | solution.py:75
  (43 shorter events, 4.0 us)
Async XLA Ops:
  7.2 8.1 %copy-start.6 = (s32[2]{0:T(128)S(1)}, s32[2]{0:T(128)}, u32[]{:S(2)}) copy-start(s32[2]{0:T(128)} %param.11) | copy-start | bytes 28
  7.2 8.2 %copy-start.4 = (f32[3,1536]{1,0:T(4,128)S(1)}, f32[3,1536]{1,0:T(4,128)}, u32[]{:S(2)}) copy-start(f32[3,1536]{1,0:T(4,128)} %param.9) | copy-start | bytes 55300
  7.2 8.3 %copy-start.5 = (s32[2,128]{1,0:T(2,128)S(1)}, s32[2,128]{1,0:T(2,128)}, u32[]{:S(2)}) copy-start(s32[2,128]{1,0:T(2,128)} %param.12) | copy-start | bytes 3076
  7.2 72.5 %all-gather.2.cloned.1.call-start = ((), (), s32[]{:S(2)}) async-start(), calls=%async_computation.1 | async-start | bytes 5308416 | tf_op jit(solution)/shard_map/all_gather | solution.py:64
  7.9 15.0 %all-to-all-start = ((bf16[16,64,192]{2,1,0:T(8,128)(2,1)}), bf16[16,64,192]{2,1,0:T(8,128)(2,1)S(1)}, u32[]{:S(2)}, u32[]{:S(2)}) async-start(bf16[16,64,192]{2,1,0:T(8,128)(2,1)} %param.7), calls=%async_computation | async-start | bytes 1048576 | tf_op jit(solution)/shard_map/all_to_all | solution.py:49
  13.3 21.4 %collective-permute-start.3 = (bf16[2,128,1536]{2,1,0:T(8,128)(2,1)}, bf16[2,128,1536]{2,1,0:T(8,128)(2,1)}, u32[]{:S(2)}, u32[]{:S(2)}) collective-permute-start(bf16[2,128,1536]{2,1,0:T(8,128)(2,1)} %param.13), channel_id=1, source_target_pairs={{0,8},{8,16},{16,24},{24,32},{32,40},{40,48},{48,56},{56,64},{64,7... | collective-permute-start | bytes 2359304 | tf_op jit(solution)/shard_map/ppermute | solution.py:26
  26.5 8.2 %copy-start = (bf16[2,128,1536]{2,1,0:T(8,128)(2,1)}, bf16[2,128,1536]{2,1,0:T(8,128)(2,1)S(1)}, u32[]{:S(2)}) copy-start(bf16[2,128,1536]{2,1,0:T(8,128)(2,1)S(1)} %add_convert_fusion) | copy-start | bytes 2359300
  26.6 13.7 %collective-permute-start = (bf16[2,1,1536]{2,1,0:T(2,128)(2,1)S(1)}, bf16[2,1,1536]{2,1,0:T(2,128)(2,1)S(1)}, u32[]{:S(2)}, u32[]{:S(2)}) collective-permute-start(bf16[2,1,1536]{2,1,0:T(2,128)(2,1)S(1)} %get-tuple-element.40), channel_id=1, source_target_pairs={{0,8},{8,16},{16,24},{24,32},{32,40},{40,48},{48,56},{56,64},{64,7... | collective-permute-start | bytes 18440 | tf_op jit(solution)/shard_map/ppermute | solution.py:17
  28.5 7.7 %copy-start.2 = (bf16[2,128,1536]{2,1,0:T(8,128)(2,1)S(1)}, bf16[2,128,1536]{2,1,0:T(8,128)(2,1)}, u32[]{:S(2)}) copy-start(bf16[2,128,1536]{2,1,0:T(8,128)(2,1)} %custom-call) | copy-start | bytes 2359300
  28.5 12.4 %collective-permute-start.1 = (bf16[2,1,1536]{2,1,0:T(2,128)(2,1)S(1)}, bf16[2,1,1536]{2,1,0:T(2,128)(2,1)S(1)}, u32[]{:S(2)}, u32[]{:S(2)}) collective-permute-start(bf16[2,1,1536]{2,1,0:T(2,128)(2,1)S(1)} %get-tuple-element.41), channel_id=1, source_target_pairs={{8,0},{16,8},{24,16},{32,24},{40,32},{48,40},{56,48},{64,56},{72,6... | collective-permute-start | bytes 18440 | tf_op jit(solution)/shard_map/ppermute | solution.py:18
  36.2 43.5 %copy-start.1 = (bf16[2,128,1536]{2,1,0:T(8,128)(2,1)S(1)}, bf16[2,128,1536]{2,1,0:T(8,128)(2,1)}, u32[]{:S(2)}) copy-start(bf16[2,128,1536]{2,1,0:T(8,128)(2,1)} %copy-done) | copy-start | bytes 2359300
  40.3 51.6 %copy-start.3 = (bf16[2,128,1536]{2,1,0:T(8,128)(2,1)}, bf16[2,128,1536]{2,1,0:T(8,128)(2,1)S(1)}, u32[]{:S(2)}) copy-start(bf16[2,128,1536]{2,1,0:T(8,128)(2,1)S(1)} %get-tuple-element.11) | copy-start | bytes 2359300
  79.7 12.1 %copy-start.7 = (bf16[1536,1536]{1,0:T(8,128)(2,1)S(1)}, bf16[1536,1536]{1,0:T(8,128)(2,1)}, u32[]{:S(2)}) copy-start(bf16[1536,1536]{1,0:T(8,128)(2,1)} %all-gather.2.cloned.1.call-done) | copy-start | bytes 14155780
  88.0 128.8 %collective-permute-start.2 = (bf16[2,128,1536]{2,1,0:T(8,128)(2,1)}, bf16[2,128,1536]{2,1,0:T(8,128)(2,1)}, u32[]{:S(2)}, u32[]{:S(2)}) collective-permute-start(bf16[2,128,1536]{2,1,0:T(8,128)(2,1)} %fusion.10), channel_id=1, source_target_pairs={{8,0},{16,8},{24,16},{32,24},{40,32},{48,40},{56,48},{64,56},{72,6... | collective-permute-start | bytes 2359304 | tf_op jit(solution)/shard_map/ppermute | solution.py:26
  200.8 5.1 %collective-permute-start.4 = (bf16[2,1,1536]{2,1,0:T(2,128)(2,1)S(1)}, bf16[2,1,1536]{2,1,0:T(2,128)(2,1)S(1)}, u32[]{:S(2)}, u32[]{:S(2)}) collective-permute-start(bf16[2,1,1536]{2,1,0:T(2,128)(2,1)S(1)} %get-tuple-element.38), channel_id=1, source_target_pairs={{8,0},{16,8},{24,16},{32,24},{40,32},{48,40},{56,48},{64,56},{72,6... | collective-permute-start | bytes 18440 | tf_op jit(solution)/shard_map/ppermute | solution.py:18
  203.0 7.4 %collective-permute-start.5 = (bf16[2,1,1536]{2,1,0:T(2,128)(2,1)S(1)}, bf16[2,1,1536]{2,1,0:T(2,128)(2,1)S(1)}, u32[]{:S(2)}, u32[]{:S(2)}) collective-permute-start(bf16[2,1,1536]{2,1,0:T(2,128)(2,1)S(1)} %get-tuple-element.39), channel_id=1, source_target_pairs={{0,8},{8,16},{16,24},{24,32},{32,40},{40,48},{48,56},{56,64},{64,7... | collective-permute-start | bytes 18440 | tf_op jit(solution)/shard_map/ppermute | solution.py:17
Sparse Core Ops, SparseCore 0:
  10.1 69.5 all-gather.1
where the time goes:
time: 227 us; the launch traced here: 226 us
  blocking collectives  106 us (47%)
  waiting for transfers between devices  52 us (23%)
  starting transfers between devices  23.8 us (10%)
  between operations  14.3 us (6%)
  matrix products  13.5 us (6%)
  other arithmetic  9.01 us (4%)
  local copies, waits for them, and re-layouts  7.43 us (3%)
    psum x1, blocking collectives, shards(): filter_sum = lax.psum(filter_terms, ('seq', 'head'))  106 us
    all_gather x1, waiting for transfers between devices, shards(): full_weight = lax.all_gather(point_weight, 'head', axis=0, tiled=True)  38.8 us
    ppermute x2, starting transfers between devices, extended(): after = lax.ppermute(initial, axis, down)  8.39 us
    dot_general x1, matrix products, shards(): jnp.dot(flat_act, full_weight, preferred_element_type=jnp.float32)  8.3 us
    all_to_all x1, waiting for transfers between devices, shards(): lax.all_to_all(attention, 'head', split_axis=0, concat_axis=2, tiled=True)  7.36 us
    ppermute x2, starting transfers between devices, passed_along(): return lax.ppermute(shard, axis, pairs)  5.71 us
    all_to_all x1, starting transfers between devices, shards(): lax.all_to_all(attention, 'head', split_axis=0, concat_axis=2, tiled=True)  5.41 us
  transfers between devices with their start and end apart: 8, of which 4 were waited for; matrix products, arithmetic and copies ran while one was open for 9% of the time, Pallas kernels for 0%

commit v1 on v0

--- a/solution.py
+++ b/solution.py
@@ -122,7 +122,7 @@
             ),
         ]
     )
-    filter_sum = lax.psum(filter_terms, ("seq", "head"))
+    filter_sum = jnp.sum(lax.all_gather(filter_terms, ("seq", "head")), axis=0)
     row_count = local_seqs * lax.axis_size("head") * slab_rows * lax.axis_size("seq")
     filter_grad = filter_sum * (1.0 / math.sqrt(row_count))
     return (target_rows, attention_grad, skip_grad, filter_grad)

time: 227 us -> 1530 us (6.74)
  the two profiles are of different devices: /device:TPU:32 before, /device:TPU:99 now
where the time goes in v1:
time: 1530 us
  waiting for transfers between devices  1440 us (94%)
  starting transfers between devices  35 us (2%)
  matrix products  15.5 us (1%)
    all_gather x1, waiting for transfers between devices, shards(): filter_sum = jnp.sum(lax.all_gather(filter_terms, ('seq', 'head')), axis=0)  1400 us
    all_gather x1, waiting for transfers between devices, shards(): full_weight = lax.all_gather(point_weight, 'head', axis=0, tiled=True)  32.2 us
  transfers between devices with their start and end apart: 9, of which 4 were waited for; matrix products, arithmetic and copies ran while one was open for 2% of the time, Pallas kernels for 0%

profile of v1, /device:TPU:99, one launch (start us, length us, event | category | flops | bytes accessed | tf_op | source)
XLA Modules:
  0.0 1532.1 jit_solution(2848588407416943695)
XLA Ops:
  7.9 5.4 all-to-all-start
  13.3 4.9 collective-permute-start.3
  18.4 2.6 all-to-all-done
  22.2 1.1 convert_element_type.67
  23.3 1.3 add_convert_fusion
  24.6 4.1 collective-permute-start.1
  28.7 11.5 collective-permute-start
  40.3 1.5 pad_maximum_fusion
  41.8 4.0 while.1
  42.4 1.4 dynamic-slice_dynamic-update-slice_fusion.2
  44.4 1.4 dynamic-slice_dynamic-update-slice_fusion.2
  45.9 32.2 %all-gather.5.cloned.1.call-done = bf16[1536,1536]{1,0:T(8,128)(2,1)} async-done(((bf16[192,1536]{1,0:T(8,128)(2,1)}), bf16[1536,1536]{1,0:T(8,128)(2,1)}) %all-gather.5.cloned.1.call-update) | async-done | bytes 4718608 | tf_op jit(solution)/shard_map/all_gather | solution.py:64
  78.0 4.9 fusion.25
  83.7 8.3 fusion.10
  91.9 2.6 collective-permute-start.2
  94.5 4.5 collective-permute-start.5
  99.0 2.1 collective-permute-start.4
  101.2 6.3 collective-permute-done.4
  107.5 1.5 fusion.111
  109.0 0.9 reshape.30
  110.0 2.8 reduce_sum.18
  112.8 2.3 convolution_convert_fusion
  115.1 1403.2 %all-gather.7.cloned.1.call-done = f32[512,3,1536]{2,1,0:T(4,128)} async-done(((f32[1,3,1536]{2,1,0:T(4,128)}), f32[512,3,1536]{2,1,0:T(4,128)}) %all-gather.7.cloned.1.call-update) | async-done | bytes 9437200 | tf_op jit(solution)/shard_map/all_gather | solution.py:125
  1518.4 6.3 reduce_sum.19
  (46 shorter events, 4.7 us)
Async XLA Ops:
  7.2 11.0 copy-start.7
  7.2 11.2 copy-start.5
  7.2 70.9 %all-gather.5.cloned.1.call-start = ((), (), s32[]{:S(2)}) async-start(), calls=%async_computation.1 | async-start | bytes 5308416 | tf_op jit(solution)/shard_map/all_gather | solution.py:64
  7.9 13.1 all-to-all-start
  13.3 1505.1 %all-gather.7.cloned.1.call-start = ((), (), s32[]{:S(2)}) async-start(), calls=%async_computation.2 | async-start | bytes 12607488 | tf_op jit(solution)/shard_map/all_gather | solution.py:125
  13.3 27.0 %collective-permute-start.3 = (bf16[2,128,1536]{2,1,0:T(8,128)(2,1)}, bf16[2,128,1536]{2,1,0:T(8,128)(2,1)}, u32[]{:S(2)}, u32[]{:S(2)}) collective-permute-start(bf16[2,128,1536]{2,1,0:T(8,128)(2,1)} %param.13), channel_id=1, source_target_pairs={{0,8},{8,16},{16,24},{24,32},{32,40},{40,48},{48,56},{56,64},{64,7... | collective-permute-start | bytes 2359304 | tf_op jit(solution)/shard_map/ppermute | solution.py:26
  24.6 15.7 %copy-start = (bf16[2,128,1536]{2,1,0:T(8,128)(2,1)}, bf16[2,128,1536]{2,1,0:T(8,128)(2,1)S(1)}, u32[]{:S(2)}) copy-start(bf16[2,128,1536]{2,1,0:T(8,128)(2,1)S(1)} %add_convert_fusion) | copy-start | bytes 2359300
  24.6 21.2 %collective-permute-start.1 = (bf16[2,1,1536]{2,1,0:T(2,128)(2,1)S(1)}, bf16[2,1,1536]{2,1,0:T(2,128)(2,1)S(1)}, u32[]{:S(2)}, u32[]{:S(2)}) collective-permute-start(bf16[2,1,1536]{2,1,0:T(2,128)(2,1)S(1)} %get-tuple-element.45), channel_id=1, source_target_pairs={{8,0},{16,8},{24,16},{32,24},{40,32},{48,40},{56,48},{64,56},{72,6... | collective-permute-start | bytes 18440 | tf_op jit(solution)/shard_map/ppermute | solution.py:18
  28.7 13.0 copy-start.2
  28.7 17.1 %collective-permute-start = (bf16[2,1,1536]{2,1,0:T(2,128)(2,1)S(1)}, bf16[2,1,1536]{2,1,0:T(2,128)(2,1)S(1)}, u32[]{:S(2)}, u32[]{:S(2)}) collective-permute-start(bf16[2,1,1536]{2,1,0:T(2,128)(2,1)S(1)} %get-tuple-element.44), channel_id=1, source_target_pairs={{0,8},{8,16},{16,24},{24,32},{32,40},{40,48},{48,56},{56,64},{64,7... | collective-permute-start | bytes 18440 | tf_op jit(solution)/shard_map/ppermute | solution.py:17
  41.8 36.2 %copy-start.1 = (bf16[2,128,1536]{2,1,0:T(8,128)(2,1)S(1)}, bf16[2,128,1536]{2,1,0:T(8,128)(2,1)}, u32[]{:S(2)}) copy-start(bf16[2,128,1536]{2,1,0:T(8,128)(2,1)} %copy-done) | copy-start | bytes 2359300
  45.8 37.1 %copy-start.3 = (bf16[2,128,1536]{2,1,0:T(8,128)(2,1)}, bf16[2,128,1536]{2,1,0:T(8,128)(2,1)S(1)}, u32[]{:S(2)}) copy-start(bf16[2,128,1536]{2,1,0:T(8,128)(2,1)S(1)} %get-tuple-element.11) | copy-start | bytes 2359300
  83.6 17.5 %copy-start.6 = (s32[2,128]{1,0:T(2,128)S(1)}, s32[2,128]{1,0:T(2,128)}, u32[]{:S(2)}) copy-start(s32[2,128]{1,0:T(2,128)} %param.12) | copy-start | bytes 3076
  83.7 23.8 %copy-start.4 = (bf16[2,128,1536]{2,1,0:T(8,128)(2,1)S(1)}, bf16[2,128,1536]{2,1,0:T(8,128)(2,1)}, u32[]{:S(2)}) copy-start(bf16[2,128,1536]{2,1,0:T(8,128)(2,1)} %copy-done.3) | copy-start | bytes 2359300
  91.9 20.9 %collective-permute-start.2 = (bf16[2,128,1536]{2,1,0:T(8,128)(2,1)}, bf16[2,128,1536]{2,1,0:T(8,128)(2,1)}, u32[]{:S(2)}, u32[]{:S(2)}) collective-permute-start(bf16[2,128,1536]{2,1,0:T(8,128)(2,1)} %fusion.10), channel_id=1, source_target_pairs={{8,0},{16,8},{24,16},{32,24},{40,32},{48,40},{56,48},{64,56},{72,6... | collective-permute-start | bytes 2359304 | tf_op jit(solution)/shard_map/ppermute | solution.py:26
  94.5 6.7 collective-permute-start.5
  99.0 8.5 collective-permute-start.4
Sparse Core Ops, SparseCore 0:
  10.1 67.8 all-gather.4
  83.8 1434.5 all-gather.6
